TPU v7x, 32 devices: a whole 2x2x4 slice. The times are simulated.
32 devices in a mesh: groups: 2 (over y), seq: 4 (over z), head: 2 (over x), sub: 2 (over core).
Axes of the slice: x: 2, y: 2, z: 4, core: 2. Of those that a mesh axis runs over, the one named last changes fastest.
Arguments:
- inputs: bfloat16 [16384, 1536], P(('groups', 'seq'), ('head', 'sub')), parts along dimension 0, may hold values from -6 to 6
- b_proj: bfloat16 [16384, 128], P(('groups', 'seq')), parts along dimension 0, may hold values from -0.109375 to 0.109375
- c_proj: bfloat16 [16384, 128], P(('groups', 'seq')), parts along dimension 0, may hold values from -6 to 6
- step_codes: int32 [24, 16384], P(('head', 'sub'), ('groups', 'seq')), parts along dimension 1, may hold values from 0 to 3
- gate_codes: int32 [16384], P(('groups', 'seq')), parts along dimension 0, may hold values from 0 to 2
- decay_rates: float32 [24], P(('head', 'sub')), may hold values from 1.8310547e-05 to 0.12
- skip_gain: float32 [24], P(('head', 'sub')), may hold values from 0.5 to 1.5
- conv_weight: float32 [4, 1536], P(None, ('head', 'sub')), may hold values from -3 to 3
- out_cotangent: bfloat16 [16384, 1536], P(('groups', 'seq'), ('head', 'sub')), parts along dimension 0, may hold values from -6 to 6
Outputs:
- layer_out: bfloat16 [16384, 1536], P(('groups', 'seq'), ('head', 'sub')), parts along dimension 0
- input_grad: bfloat16 [16384, 1536], P(('groups', 'seq'), ('head', 'sub')), parts along dimension 0
- conv_grad: float32 [8, 1536], P('groups', ('head', 'sub')), parts along dimension 0
There are 2 independent parts, one for each index of `groups`. A program takes and returns all parts, laid end to end along the dimension named above; an argument that names none is the same for every part. Nothing has to cross between parts.
All inputs are finite; a program needn't handle non-finite values.
Results may differ from a plain program's by a relative error of at most 0.0062.
Values may be sent and summed in bfloat16 or wider, within the bound.
No kernel may reach another device: no remote copies, remote signals or barrier semaphores. Data moves between devices by JAX's collectives and lax.ppermute only.
A program may use at most 64 MiB of HBM per device.

v0:
```python
import jax
import jax.numpy as jnp
from jax import lax
from jax.sharding import PartitionSpec as P

BLOCK = 512


def shifted(block, axis, distance):
    devices = range(lax.axis_size(axis))
    route = [(i - distance, i) for i in devices if i - distance in devices]
    return lax.ppermute(block, axis, route)


def shards(
    inputs,
    b_proj,
    c_proj,
    step_codes,
    gate_codes,
    decay_rates,
    skip_gain,
    conv_weight,
    out_cotangent,
):
    row_count, channels = inputs.shape
    conv_taps = conv_weight.shape[0]
    head_count = decay_rates.shape[0]
    head_width = channels // head_count
    state_width = b_proj.shape[1]
    block_count = row_count // BLOCK
    highest = lax.Precision.HIGHEST
    before_rows = shifted(inputs[row_count - (conv_taps - 1) :], "seq", 1)
    padded = jnp.concatenate([before_rows, inputs], axis=0)
    preact = jnp.zeros((row_count, channels), jnp.float32)
    for offset in range(conv_taps):
        preact = preact + conv_weight[offset] * padded[offset : offset + row_count].astype(
            jnp.float32
        )
    mixed_in = jax.nn.silu(preact).astype(jnp.bfloat16)
    step_size = jnp.exp2(-step_codes.astype(jnp.float32))
    log_decay = (
        -decay_rates[:, None] * step_size
        + jnp.log(1.0 - gate_codes.astype(jnp.float32) / 4.0)[None, :]
    )
    cum_decay = jnp.cumsum(log_decay.reshape(head_count, block_count, BLOCK), axis=-1).transpose(
        1, 0, 2
    )
    step_blocks = step_size.reshape(head_count, block_count, BLOCK).transpose(1, 0, 2)
    mixed_blocks = mixed_in.reshape(block_count, BLOCK, head_count, head_width)
    grad_blocks = out_cotangent.reshape(block_count, BLOCK, head_count, head_width)
    b_blocks = b_proj.reshape(block_count, BLOCK, state_width)
    c_blocks = c_proj.reshape(block_count, BLOCK, state_width)
    causal = jnp.arange(BLOCK)[:, None] >= jnp.arange(BLOCK)[None, :]

    def local_block(unused, block_data):
        mixed_b, grad_b, b_block, c_block, cum_block, step_block = block_data
        scores = jnp.dot(c_block, b_block.T, preferred_element_type=jnp.float32)
        spread = cum_block[:, :, None] - cum_block[:, None, :]
        decays = jnp.exp(jnp.where(causal[None], spread, -jnp.inf))
        weights = (scores[None] * decays * step_block[:, None, :]).astype(jnp.bfloat16)
        ahead_part = jnp.einsum(
            "hts,shp->thp", weights, mixed_b, preferred_element_type=jnp.float32
        )
        behind_part = jnp.einsum(
            "hst,shp->thp", weights, grad_b, preferred_element_type=jnp.float32
        )
        block_total = cum_block[:, -1]
        in_factor = (jnp.exp(block_total[:, None] - cum_block) * step_block).T
        scaled_in = (mixed_b.astype(jnp.float32) * in_factor[:, :, None]).astype(jnp.bfloat16)
        fresh_state = jnp.einsum(
            "thp,tn->hpn", scaled_in, b_block, preferred_element_type=jnp.float32
        )
        scaled_out = (grad_b.astype(jnp.float32) * jnp.exp(cum_block).T[:, :, None]).astype(
            jnp.bfloat16
        )
        fresh_adjoint = jnp.einsum(
            "thp,tn->hpn", scaled_out, c_block, preferred_element_type=jnp.float32
        )
        return (unused, (ahead_part, behind_part, fresh_state, fresh_adjoint))

    unused_carry, block_results = lax.scan(
        local_block,
        jnp.zeros((), jnp.float32),
        (mixed_blocks, grad_blocks, b_blocks, c_blocks, cum_decay, step_blocks),
    )
    ahead_parts, behind_parts, fresh_states, fresh_adjoints = block_results
    block_totals = cum_decay[:, :, -1]
    zero_state = jnp.zeros((head_count, head_width, state_width), jnp.float32)
    running = zero_state
    start_list = []
    for block_index in range(block_count):
        start_list.append(running)
        running = (
            jnp.exp(block_totals[block_index])[:, None, None] * running + fresh_states[block_index]
        )
    local_end = running
    running = zero_state
    later_list = []
    for block_index in range(block_count - 1, -1, -1):
        later_list.append(running)
        running = (
            jnp.exp(block_totals[block_index])[:, None, None] * running
            + fresh_adjoints[block_index]
        )
    end_list = later_list[::-1]
    device_total = jnp.sum(block_totals, axis=0)
    totals_all = lax.all_gather(device_total[None], "seq", axis=0, tiled=True)
    position = lax.axis_index("seq")
    prefix = jnp.cumsum(totals_all, axis=0) - totals_all
    own_prefix = lax.dynamic_slice_in_dim(prefix, position, 1, 0)[0]
    end_pieces = lax.all_gather(local_end[None], "seq", axis=0, tiled=True)
    start_pieces = lax.all_gather(running[None], "seq", axis=0, tiled=True)
    piece_count = end_pieces.shape[0]
    sources = jnp.arange(piece_count, dtype=jnp.int32)
    from_below = (sources < position)[:, None]
    from_above = (sources > position)[:, None]
    forward_weight = jnp.exp(
        jnp.where(from_below, own_prefix[None] - prefix - totals_all, -jnp.inf)
    )
    backward_weight = jnp.exp(
        jnp.where(from_above, prefix - own_prefix[None] - device_total[None], -jnp.inf)
    )
    forward_sum = jnp.einsum("jh,jhpn->hpn", forward_weight, end_pieces, precision=highest)
    backward_sum = jnp.einsum("jh,jhpn->hpn", backward_weight, start_pieces, precision=highest)
    before_blocks = jnp.cumsum(block_totals, axis=0) - block_totals
    after_blocks = device_total[None] - jnp.cumsum(block_totals, axis=0)
    start_states = jnp.exp(before_blocks)[:, :, None, None] * forward_sum[None] + jnp.stack(
        start_list
    )
    end_adjoints = jnp.exp(after_blocks)[:, :, None, None] * backward_sum[None] + jnp.stack(
        end_list
    )
    carried_out = jnp.einsum(
        "btn,bhpn->bthp",
        c_blocks,
        start_states.astype(jnp.bfloat16),
        preferred_element_type=jnp.float32,
    )
    carried_out = carried_out * jnp.exp(cum_decay).transpose(0, 2, 1)[..., None]
    skip_wide = skip_gain[None, None, :, None]
    layer_out = (skip_wide * mixed_blocks.astype(jnp.float32) + ahead_parts + carried_out).astype(
        jnp.bfloat16
    )
    layer_out = layer_out.reshape(row_count, channels)
    back_factor = (step_blocks * jnp.exp(block_totals[:, :, None] - cum_decay)).transpose(0, 2, 1)
    carried_back = jnp.einsum(
        "btn,bhpn->bthp",
        b_blocks,
        end_adjoints.astype(jnp.bfloat16),
        preferred_element_type=jnp.float32,
    )
    carried_back = carried_back * back_factor[..., None]
    grad_in = (skip_wide * grad_blocks.astype(jnp.float32) + behind_parts + carried_back).reshape(
        row_count, channels
    )
    gate_value = jax.nn.sigmoid(preact)
    grad_pre = grad_in * gate_value * (1.0 + preact * (1.0 - gate_value))
    after_rows = shifted(grad_pre[: conv_taps - 1], "seq", -1)
    extended = jnp.concatenate([grad_pre, after_rows], axis=0)
    input_grad = jnp.zeros((row_count, channels), jnp.float32)
    for offset in range(conv_taps):
        shift_from = conv_taps - 1 - offset
        input_grad = (
            input_grad + conv_weight[offset] * extended[shift_from : shift_from + row_count]
        )
    tap_sums = [
        jnp.sum(grad_pre * padded[offset : offset + row_count].astype(jnp.float32), axis=0)
        for offset in range(conv_taps)
    ]
    local_grad = jnp.stack(tap_sums)
    conv_grad = lax.psum(local_grad, "seq") * (row_count * lax.axis_size("seq")) ** (-0.5)
    return (layer_out, input_grad.astype(jnp.bfloat16), conv_grad)


def solution(mesh):
    in_specs = (
        P(("groups", "seq"), ("head", "sub")),
        P(("groups", "seq"), None),
        P(("groups", "seq"), None),
        P(("head", "sub"), ("groups", "seq")),
        P(("groups", "seq")),
        P(("head", "sub")),
        P(("head", "sub")),
        P(None, ("head", "sub")),
        P(("groups", "seq"), ("head", "sub")),
    )
    out_specs = (
        P(("groups", "seq"), ("head", "sub")),
        P(("groups", "seq"), ("head", "sub")),
        P("groups", ("head", "sub")),
    )
    return jax.shard_map(shards, mesh=mesh, in_specs=in_specs, out_specs=out_specs, check_vma=False)
```

profile of v0, /device:TPU:0, one launch (start us, length us, event | category | flops | bytes accessed | tf_op | source)
XLA Modules:
  0.0 186.4 jit_solution(6552634328493133739)
XLA Ops:
  2.2 4.9 %collective-permute-start = (bf16[3,384]{0,1:T(8,128)(2,1)}, bf16[3,384]{0,1:T(8,128)(2,1)S(1)}, u32[]{:S(2)}, u32[]{:S(2)}) collective-permute-start(bf16[3,384]{0,1:T(8,128)(2,1)} %copy.102), channel_id=1, source_target_pairs={{0,4},{4,8},{8,12},{1,5},{5,9},{9,13},{2,6},{6,10},{10,14},{3,7},{... | collective-permute-start | bytes 6920 | tf_op jit(solution)/shard_map/ppermute | solution.py:12
  9.5 7.2 %reduce-window.6 = f32[6,4,4,128]{3,2,1,0:T(4,128)S(1)} reduce-window(f32[6,4,4,128]{3,2,1,0:T(4,128)S(1)} %reshape.125, f32[]{:T(128)} %constant.51.clone.1), window={size=1x1x1x128 pad=0_0x0_0x0_0x127_0}, to_apply=%region_0.1 | reduce-window | flops 1560576 | bytes 98308 | tf_op jit(solution)/shard_map/reduce-window
  18.6 1.2 dynamic-slice
  20.7 9.9 %all-reduce = f32[24]{0:T(128)S(1)} all-reduce(f32[24]{0:T(128)S(1)} %dynamic-update-slice), channel_id=2, replica_groups=mesh['groups'=2,'seq'=4,'head'=2,'sub'=2] {'seq'}, use_global_device_ids=true, to_apply=%add | all-reduce | flops 24 | bytes 192
  32.4 1.7 copy.103
  34.2 1.7 copy.108
  35.9 2.9 %reshape.128 = bf16[4,512,6,64]{1,0,3,2:T(4,128)(2,1)S(1)} reshape(bf16[2048,384]{0,1:T(8,128)(2,1)} %copy.108) | data formatting | bytes 3145728 | tf_op jit(solution)/shard_map/reshape | solution.py:51
  38.8 1.7 copy.112
  40.7 4.2 %multiply_convert_fusion.13 = (bf16[2048,384]{0,1:T(8,128)(2,1)}, f32[2048,384]{0,1:T(8,128)}) fusion(bf16[2048,384]{0,1:T(8,128)(2,1)S(1)} %copy.103, f32[384]{0:T(512)S(1)} %get-tuple-element.162, bf16[3,384]{0,1:T(8,128)(2,1)S(1)} %collective-permute-done, f32[384]{0:T(512)S(1)} %get-tuple-element.163, f32[384]{0:T(512)S(1)} %get-tuple-element.161, ...), kind=kLoop, calls=%fused_computation.84 | loop fusion | flops 19660800 | bytes 6299904 | tf_op jit(solution)/shard_map/convert_element_type | solution.py:40
  44.9 2.9 %reshape.122 = bf16[4,512,6,64]{1,0,3,2:T(4,128)(2,1)S(1)} reshape(bf16[2048,384]{0,1:T(8,128)(2,1)} %get-tuple-element.195) | data formatting | bytes 3145728 | tf_op jit(solution)/shard_map/reshape | solution.py:50
  47.9 1.5 copy.105
  49.4 55.1 %while.17 = (s32[]{:T(128)}, f32[4,512,6,64]{1,3,2,0:T(8,128)}, f32[4,512,6,64]{1,3,2,0:T(8,128)}, f32[4,6,64,128]{3,2,1,0:T(8,128)}, f32[4,6,64,128]{3,2,1,0:T(...) while((s32[]{:T(128)}, f32[4,512,6,64]{1,3,2,0:T(8,128)}, ...), condition=%wide.region_3.4_spmd.clone, body=%wide.region_2.3_spmd.clone.sunk | while | flops 587601920 | bytes 8374465 | solution.py:82
  49.4 1.2 fusion.106
  50.8 3.9 %fusion.108 = f32[4,512,6,64]{1,3,2,0:T(8,128)} fusion(f32[4,512,6,64]{1,3,2,0:T(8,128)} %get-tuple-element.310, s32[]{:T(128)} %get-tuple-element.308, f32[6,512]{1,0:T(8,128)S(1)} %bitcast.175, f32[6,512]{1,0:T(8,128)S(1)} %bitcast.177, f32[512,512]{1,0:T(8,128)S(1)} %fusion.106, pred[512,512]{1,0:T(8,128)(4,1)S(1)} %iota_compare_fusion.4, ...), kind=kOutput, calls=%fused_computation.7.clone.1 | convolution fusion | flops 209190912 | bytes 2540544 | tf_op jit(solution)/shard_map/while/body/eval_jaxpr/hst,shp->thp/dot_general | solution.py:65
  54.7 3.9 %fusion.107 = f32[4,512,6,64]{1,3,2,0:T(8,128)} fusion(f32[4,512,6,64]{1,3,2,0:T(8,128)} %get-tuple-element.309, s32[]{:T(128)} %get-tuple-element.308, f32[6,512]{1,0:T(8,128)S(1)} %bitcast.176, f32[6,512]{1,0:T(8,128)S(1)} %bitcast.178, f32[512,512]{1,0:T(8,128)S(1)} %fusion.106, pred[512,512]{1,0:T(8,128)(4,1)S(1)} %iota_compare_fusion.4, ...), kind=kOutput, calls=%fused_computation.5.clone.1 | convolution fusion | flops 209190912 | bytes 2540544 | tf_op jit(solution)/shard_map/while/body/eval_jaxpr/hts,shp->thp/dot_general | solution.py:62
  59.1 2.0 %fusion.109 = f32[4,6,64,128]{3,2,1,0:T(8,128)} fusion(f32[4,6,64,128]{3,2,1,0:T(8,128)} %get-tuple-element.311, s32[]{:T(128)} %get-tuple-element.308, f32[512,6]{0,1:T(8,128)S(1)} %copy.156, bf16[4,512,6,64]{1,3,2,0:T(8,128)(2,1)} %get-tuple-element.325, bf16[4,512,128]{2,1,0:T(8,128)(2,1)} %get-tuple-element.327), kind=kOutput, calls=%fused_computation.11.clone.1 | convolution fusion | flops 50921472 | bytes 734720 | tf_op jit(solution)/shard_map/while/body/eval_jaxpr/thp,tn->hpn/dot_general | solution.py:71
  61.2 2.0 %fusion.110 = f32[4,6,64,128]{3,2,1,0:T(8,128)} fusion(f32[4,6,64,128]{3,2,1,0:T(8,128)} %get-tuple-element.312, s32[]{:T(128)} %get-tuple-element.308, f32[512,6]{0,1:T(8,128)S(1)} %copy.157, bf16[4,512,6,64]{1,3,2,0:T(8,128)(2,1)} %get-tuple-element.330, bf16[4,512,128]{2,1,0:T(8,128)(2,1)S(1)} %get-tuple-element.326), kind=kOutput, calls=%fused_computation.9.clone.1 | convolution fusion | flops 50921472 | bytes 738816 | tf_op jit(solution)/shard_map/while/body/eval_jaxpr/thp,tn->hpn/dot_general | solution.py:77
  64.5 3.9 %fusion.108 = f32[4,512,6,64]{1,3,2,0:T(8,128)} fusion(f32[4,512,6,64]{1,3,2,0:T(8,128)} %get-tuple-element.310, s32[]{:T(128)} %get-tuple-element.308, f32[6,512]{1,0:T(8,128)S(1)} %bitcast.175, f32[6,512]{1,0:T(8,128)S(1)} %bitcast.177, f32[512,512]{1,0:T(8,128)S(1)} %fusion.106, pred[512,512]{1,0:T(8,128)(4,1)S(1)} %iota_compare_fusion.4, ...), kind=kOutput, calls=%fused_computation.7.clone.1 | convolution fusion | flops 209190912 | bytes 2540544 | tf_op jit(solution)/shard_map/while/body/eval_jaxpr/hst,shp->thp/dot_general | solution.py:65
  68.4 3.9 %fusion.107 = f32[4,512,6,64]{1,3,2,0:T(8,128)} fusion(f32[4,512,6,64]{1,3,2,0:T(8,128)} %get-tuple-element.309, s32[]{:T(128)} %get-tuple-element.308, f32[6,512]{1,0:T(8,128)S(1)} %bitcast.176, f32[6,512]{1,0:T(8,128)S(1)} %bitcast.178, f32[512,512]{1,0:T(8,128)S(1)} %fusion.106, pred[512,512]{1,0:T(8,128)(4,1)S(1)} %iota_compare_fusion.4, ...), kind=kOutput, calls=%fused_computation.5.clone.1 | convolution fusion | flops 209190912 | bytes 2540544 | tf_op jit(solution)/shard_map/while/body/eval_jaxpr/hts,shp->thp/dot_general | solution.py:62
  72.8 2.0 %fusion.109 = f32[4,6,64,128]{3,2,1,0:T(8,128)} fusion(f32[4,6,64,128]{3,2,1,0:T(8,128)} %get-tuple-element.311, s32[]{:T(128)} %get-tuple-element.308, f32[512,6]{0,1:T(8,128)S(1)} %copy.156, bf16[4,512,6,64]{1,3,2,0:T(8,128)(2,1)} %get-tuple-element.325, bf16[4,512,128]{2,1,0:T(8,128)(2,1)} %get-tuple-element.327), kind=kOutput, calls=%fused_computation.11.clone.1 | convolution fusion | flops 50921472 | bytes 734720 | tf_op jit(solution)/shard_map/while/body/eval_jaxpr/thp,tn->hpn/dot_general | solution.py:71
  74.9 2.0 %fusion.110 = f32[4,6,64,128]{3,2,1,0:T(8,128)} fusion(f32[4,6,64,128]{3,2,1,0:T(8,128)} %get-tuple-element.312, s32[]{:T(128)} %get-tuple-element.308, f32[512,6]{0,1:T(8,128)S(1)} %copy.157, bf16[4,512,6,64]{1,3,2,0:T(8,128)(2,1)} %get-tuple-element.330, bf16[4,512,128]{2,1,0:T(8,128)(2,1)S(1)} %get-tuple-element.326), kind=kOutput, calls=%fused_computation.9.clone.1 | convolution fusion | flops 50921472 | bytes 738816 | tf_op jit(solution)/shard_map/while/body/eval_jaxpr/thp,tn->hpn/dot_general | solution.py:77
  76.8 1.2 fusion.106
  78.2 4.0 %fusion.108 = f32[4,512,6,64]{1,3,2,0:T(8,128)} fusion(f32[4,512,6,64]{1,3,2,0:T(8,128)} %get-tuple-element.310, s32[]{:T(128)} %get-tuple-element.308, f32[6,512]{1,0:T(8,128)S(1)} %bitcast.175, f32[6,512]{1,0:T(8,128)S(1)} %bitcast.177, f32[512,512]{1,0:T(8,128)S(1)} %fusion.106, pred[512,512]{1,0:T(8,128)(4,1)S(1)} %iota_compare_fusion.4, ...), kind=kOutput, calls=%fused_computation.7.clone.1 | convolution fusion | flops 209190912 | bytes 2540544 | tf_op jit(solution)/shard_map/while/body/eval_jaxpr/hst,shp->thp/dot_general | solution.py:65
  82.1 3.9 %fusion.107 = f32[4,512,6,64]{1,3,2,0:T(8,128)} fusion(f32[4,512,6,64]{1,3,2,0:T(8,128)} %get-tuple-element.309, s32[]{:T(128)} %get-tuple-element.308, f32[6,512]{1,0:T(8,128)S(1)} %bitcast.176, f32[6,512]{1,0:T(8,128)S(1)} %bitcast.178, f32[512,512]{1,0:T(8,128)S(1)} %fusion.106, pred[512,512]{1,0:T(8,128)(4,1)S(1)} %iota_compare_fusion.4, ...), kind=kOutput, calls=%fused_computation.5.clone.1 | convolution fusion | flops 209190912 | bytes 2540544 | tf_op jit(solution)/shard_map/while/body/eval_jaxpr/hts,shp->thp/dot_general | solution.py:62
  86.6 2.0 %fusion.109 = f32[4,6,64,128]{3,2,1,0:T(8,128)} fusion(f32[4,6,64,128]{3,2,1,0:T(8,128)} %get-tuple-element.311, s32[]{:T(128)} %get-tuple-element.308, f32[512,6]{0,1:T(8,128)S(1)} %copy.156, bf16[4,512,6,64]{1,3,2,0:T(8,128)(2,1)} %get-tuple-element.325, bf16[4,512,128]{2,1,0:T(8,128)(2,1)} %get-tuple-element.327), kind=kOutput, calls=%fused_computation.11.clone.1 | convolution fusion | flops 50921472 | bytes 734720 | tf_op jit(solution)/shard_map/while/body/eval_jaxpr/thp,tn->hpn/dot_general | solution.py:71
  88.7 2.0 %fusion.110 = f32[4,6,64,128]{3,2,1,0:T(8,128)} fusion(f32[4,6,64,128]{3,2,1,0:T(8,128)} %get-tuple-element.312, s32[]{:T(128)} %get-tuple-element.308, f32[512,6]{0,1:T(8,128)S(1)} %copy.157, bf16[4,512,6,64]{1,3,2,0:T(8,128)(2,1)} %get-tuple-element.330, bf16[4,512,128]{2,1,0:T(8,128)(2,1)S(1)} %get-tuple-element.326), kind=kOutput, calls=%fused_computation.9.clone.1 | convolution fusion | flops 50921472 | bytes 738816 | tf_op jit(solution)/shard_map/while/body/eval_jaxpr/thp,tn->hpn/dot_general | solution.py:77
  92.0 4.0 %fusion.108 = f32[4,512,6,64]{1,3,2,0:T(8,128)} fusion(f32[4,512,6,64]{1,3,2,0:T(8,128)} %get-tuple-element.310, s32[]{:T(128)} %get-tuple-element.308, f32[6,512]{1,0:T(8,128)S(1)} %bitcast.175, f32[6,512]{1,0:T(8,128)S(1)} %bitcast.177, f32[512,512]{1,0:T(8,128)S(1)} %fusion.106, pred[512,512]{1,0:T(8,128)(4,1)S(1)} %iota_compare_fusion.4, ...), kind=kOutput, calls=%fused_computation.7.clone.1 | convolution fusion | flops 209190912 | bytes 2540544 | tf_op jit(solution)/shard_map/while/body/eval_jaxpr/hst,shp->thp/dot_general | solution.py:65
  96.0 3.9 %fusion.107 = f32[4,512,6,64]{1,3,2,0:T(8,128)} fusion(f32[4,512,6,64]{1,3,2,0:T(8,128)} %get-tuple-element.309, s32[]{:T(128)} %get-tuple-element.308, f32[6,512]{1,0:T(8,128)S(1)} %bitcast.176, f32[6,512]{1,0:T(8,128)S(1)} %bitcast.178, f32[512,512]{1,0:T(8,128)S(1)} %fusion.106, pred[512,512]{1,0:T(8,128)(4,1)S(1)} %iota_compare_fusion.4, ...), kind=kOutput, calls=%fused_computation.5.clone.1 | convolution fusion | flops 209190912 | bytes 2540544 | tf_op jit(solution)/shard_map/while/body/eval_jaxpr/hts,shp->thp/dot_general | solution.py:62
  100.4 2.0 %fusion.109 = f32[4,6,64,128]{3,2,1,0:T(8,128)} fusion(f32[4,6,64,128]{3,2,1,0:T(8,128)} %get-tuple-element.311, s32[]{:T(128)} %get-tuple-element.308, f32[512,6]{0,1:T(8,128)S(1)} %copy.156, bf16[4,512,6,64]{1,3,2,0:T(8,128)(2,1)} %get-tuple-element.325, bf16[4,512,128]{2,1,0:T(8,128)(2,1)} %get-tuple-element.327), kind=kOutput, calls=%fused_computation.11.clone.1 | convolution fusion | flops 50921472 | bytes 734720 | tf_op jit(solution)/shard_map/while/body/eval_jaxpr/thp,tn->hpn/dot_general | solution.py:71
  102.5 1.9 %fusion.110 = f32[4,6,64,128]{3,2,1,0:T(8,128)} fusion(f32[4,6,64,128]{3,2,1,0:T(8,128)} %get-tuple-element.312, s32[]{:T(128)} %get-tuple-element.308, f32[512,6]{0,1:T(8,128)S(1)} %copy.157, bf16[4,512,6,64]{1,3,2,0:T(8,128)(2,1)} %get-tuple-element.330, bf16[4,512,128]{2,1,0:T(8,128)(2,1)S(1)} %get-tuple-element.326), kind=kOutput, calls=%fused_computation.9.clone.1 | convolution fusion | flops 50921472 | bytes 738816 | tf_op jit(solution)/shard_map/while/body/eval_jaxpr/thp,tn->hpn/dot_general | solution.py:77
  104.5 1.8 slice_add_fusion
  106.3 17.3 %all_gather.11 = f32[4,6,64,128]{3,2,1,0:T(8,128)S(1)} all-gather(f32[1,6,64,128]{3,2,1,0:T(8,128)S(1)} %get-tuple-element.187), channel_id=1, replica_groups=mesh['groups'=2,'seq'=4,'head'=2,'sub'=2] {'seq'}, dimensions={0}, use_global_device_ids=true | all-gather | bytes 983040 | tf_op jit(solution)/shard_map/all_gather | solution.py:113
  123.6 1.8 fusion.62
  125.5 2.2 %fusion.55 = f32[4,512,6,64]{1,3,2,0:T(8,128)S(1)} fusion(f32[4,512,6,64]{1,3,2,0:T(8,128)S(1)} %copy-done.7, bf16[4,512,128,1]{2,1,3,0:T(8,128)(2,1)} %bitcast.19, f32[4,512,6]{1,2,0:T(8,128)S(1)} %copy.118, f32[6]{0:T(128)S(1)} %copy-done.17, f32[1,6,64,128]{3,2,1,0:T(8,128)S(1)} %broadcast.73, f32[1,6,64,128]{3,2,1,0:T(8,128)S(1)} %get-tuple-element.190, ...), kind=kOutput, calls=%fused_computation.79 | convolution fusion | flops 206438400 | bytes 9420920 | tf_op jit(solution)/shard_map/btn,bhpn->bthp/dot_general | solution.py:147
  127.7 2.0 %copy.119 = f32[4,512,6,64]{1,0,3,2:T(4,128)S(1)} copy(f32[4,512,6,64]{1,3,2,0:T(8,128)S(1)} %fusion.55) | data formatting | bytes 6291456 | tf_op jit(solution)/shard_map/add | solution.py:154
  129.7 1.5 copy.135
  132.1 4.2 %fusion.50 = (f32[384]{0:T(512)S(1)}, f32[384]{0:T(512)S(1)}, f32[384]{0:T(512)S(1)}, f32[384]{0:T(512)S(1)}, f32[2048,384]{0,1:T(8,128)}) fusion(bf16[2048,384]{0,1:T(8,128)(2,1)S(1)} %copy-done.1, bf16[3,384]{0,1:T(8,128)(2,1)S(1)} %collective-permute-done, f32[2048,384]{0,1:T(8,128)S(1)} %copy-done.5, f32[2048,384]{0,1:T(8,128)S(1)} %bitcast.164), kind=kLoop, calls=%fused_computation.72 | loop fusion | flops 22804992 | bytes 11018496 | tf_op jit(solution)/shard_map/reduce_sum | solution.py:168
  136.3 10.1 %psum.7 = f32[4,384]{1,0:T(4,128)S(1)} all-reduce(f32[4,384]{1,0:T(4,128)S(1)} %pad_maximum_fusion.2), channel_id=1, replica_groups=mesh['groups'=2,'seq'=4,'head'=2,'sub'=2] {'seq'}, use_global_device_ids=true, to_apply=%region_11.12 | all-reduce | flops 1536 | bytes 12288 | tf_op jit(solution)/shard_map/psum | solution.py:172
  146.5 1.6 slice.143
  148.1 1.3 collective-permute-start.1
  149.4 18.7 %all_gather.10 = f32[4,6,64,128]{3,2,1,0:T(8,128)S(1)} all-gather(f32[1,6,64,128]{3,2,1,0:T(8,128)S(1)} %get-tuple-element.211), channel_id=1, replica_groups=mesh['groups'=2,'seq'=4,'head'=2,'sub'=2] {'seq'}, dimensions={0}, use_global_device_ids=true | all-gather | bytes 983040 | tf_op jit(solution)/shard_map/all_gather | solution.py:112
  168.0 1.8 fusion.64
  169.9 3.0 %fusion.57 = bf16[4,512,6,64]{1,3,2,0:T(8,128)(2,1)S(1)} fusion(f32[4,512,6,64]{1,3,2,0:T(8,128)} %get-tuple-element.68, bf16[4,512,128,1]{2,1,3,0:T(8,128)(2,1)S(1)} %bitcast.166, f32[4,512,6]{1,2,0:T(8,128)S(1)} %copy.114, f32[6]{0:T(128)S(1)} %copy-done.17, f32[1,6,64,128]{3,2,1,0:T(8,128)S(1)} %get-tuple-element.212, ...), kind=kOutput, calls=%fused_computation.82 | convolution fusion | flops 207224832 | bytes 7848056 | tf_op jit(solution)/shard_map/btn,bhpn->bthp/dot_general | solution.py:134
  173.4 1.2 copy.115
  174.6 1.6 copy.134
  176.2 2.6 %copy.120 = bf16[2048,384]{1,0:T(8,128)(2,1)} copy(bf16[2048,384]{0,1:T(8,128)(2,1)} %bitcast.168) | data formatting | bytes 3145728
  178.8 5.0 %fusion.44 = bf16[2048,384]{0,1:T(8,128)(2,1)} fusion(f32[2048,384]{0,1:T(8,128)S(1)} %copy-done.4, f32[3,384]{0,1:T(8,128)S(1)} %collective-permute-done.1, f32[384]{0:T(512)S(1)} %get-tuple-element.162, f32[384]{0:T(512)S(1)} %get-tuple-element.163, f32[384]{0:T(512)S(1)} %get-tuple-element.161, f32[384]{0:T(512)S(1)} %get-tuple-element.160), kind=kLoop, calls=%fused_computation.66 | loop fusion | flops 8650752 | bytes 4729344 | tf_op jit(solution)/shard_map/convert_element_type | solution.py:173
  183.8 2.6 %copy.121 = bf16[2048,384]{1,0:T(8,128)(2,1)} copy(bf16[2048,384]{0,1:T(8,128)(2,1)} %fusion.44) | data formatting | bytes 3145728
  (125 shorter events, 14.7 us)
Async XLA Ops:
  0.6 33.6 %copy-start.8 = (bf16[2048,384]{1,0:T(8,128)(2,1)S(1)}, bf16[2048,384]{1,0:T(8,128)(2,1)}, u32[]{:S(2)}) copy-start(bf16[2048,384]{1,0:T(8,128)(2,1)} %param.19) | copy-start | bytes 4718596
  2.2 38.4 %collective-permute-start = (bf16[3,384]{0,1:T(8,128)(2,1)}, bf16[3,384]{0,1:T(8,128)(2,1)S(1)}, u32[]{:S(2)}, u32[]{:S(2)}) collective-permute-start(bf16[3,384]{0,1:T(8,128)(2,1)} %copy.102), channel_id=1, source_target_pairs={{0,4},{4,8},{8,12},{1,5},{5,9},{9,13},{2,6},{6,10},{10,14},{3,7},{... | collective-permute-start | bytes 6920 | tf_op jit(solution)/shard_map/ppermute | solution.py:12
  18.1 13.4 %copy-start.9 = (f32[6]{0:T(128)}, f32[6]{0:T(128)S(1)}, u32[]{:S(2)}) copy-start(f32[6]{0:T(128)S(1)} %get-tuple-element.156) | copy-start | bytes 76
  18.1 13.4 %copy-start.11 = (f32[6]{0:T(128)}, f32[6]{0:T(128)S(1)}, u32[]{:S(2)}) copy-start(f32[6]{0:T(128)S(1)} %get-tuple-element.157) | copy-start | bytes 76
  34.2 6.5 %copy-start = (bf16[2048,384]{0,1:T(8,128)(2,1)}, bf16[2048,384]{0,1:T(8,128)(2,1)S(1)}, u32[]{:S(2)}) copy-start(bf16[2048,384]{0,1:T(8,128)(2,1)S(1)} %copy.103) | copy-start | bytes 4718596
  38.8 6.1 %copy-start.2 = (bf16[4,512,6,64]{1,0,3,2:T(4,128)(2,1)}, bf16[4,512,6,64]{1,0,3,2:T(4,128)(2,1)S(1)}, u32[]{:S(2)}) copy-start(bf16[4,512,6,64]{1,0,3,2:T(4,128)(2,1)S(1)} %reshape.128) | copy-start | bytes 4718596
  44.9 4.4 %copy-start.6 = (bf16[2048,128]{1,0:T(8,128)(2,1)S(1)}, bf16[2048,128]{1,0:T(8,128)(2,1)}, u32[]{:S(2)}) copy-start(bf16[2048,128]{1,0:T(8,128)(2,1)} %param.13) | copy-start | bytes 1572868
  49.3 55.1 %copy-start.10 = (f32[6]{0:T(128)S(1)}, f32[6]{0:T(128)}, u32[]{:S(2)}) copy-start(f32[6]{0:T(128)} %copy-done.9) | copy-start | bytes 76
  49.4 55.1 %copy-start.12 = (f32[6]{0:T(128)S(1)}, f32[6]{0:T(128)}, u32[]{:S(2)}) copy-start(f32[6]{0:T(128)} %copy-done.11) | copy-start | bytes 76
  49.4 55.1 %copy-start.13 = (f32[6]{0:T(128)S(1)}, f32[6]{0:T(128)}, u32[]{:S(2)}) copy-start(f32[6]{0:T(128)} %get-tuple-element.158) | copy-start | bytes 76
  49.4 55.1 %copy-start.14 = (f32[6]{0:T(128)S(1)}, f32[6]{0:T(128)}, u32[]{:S(2)}) copy-start(f32[6]{0:T(128)} %get-tuple-element.159) | copy-start | bytes 76
  49.4 55.1 %copy-start.15 = (f32[6]{0:T(128)S(1)}, f32[6]{0:T(128)}, u32[]{:S(2)}) copy-start(f32[6]{0:T(128)} %get-tuple-element.217) | copy-start | bytes 76
  49.4 55.1 %copy-start.16 = (f32[6]{0:T(128)S(1)}, f32[6]{0:T(128)}, u32[]{:S(2)}) copy-start(f32[6]{0:T(128)} %get-tuple-element.218) | copy-start | bytes 76
  104.5 21.0 %copy-start.3 = (bf16[4,512,6,64]{1,0,3,2:T(4,128)(2,1)S(1)}, bf16[4,512,6,64]{1,0,3,2:T(4,128)(2,1)}, u32[]{:S(2)}) copy-start(bf16[4,512,6,64]{1,0,3,2:T(4,128)(2,1)} %copy-done.2) | copy-start | bytes 4718596
  104.5 21.0 %copy-start.7 = (f32[4,512,6,64]{1,3,2,0:T(8,128)S(1)}, f32[4,512,6,64]{1,3,2,0:T(8,128)}, u32[]{:S(2)}) copy-start(f32[4,512,6,64]{1,3,2,0:T(8,128)} %get-tuple-element.70) | copy-start | bytes 9437188
  104.5 21.0 %copy-start.17 = (f32[6]{0:T(128)S(1)}, f32[6]{0:T(128)}, u32[]{:S(2)}) copy-start(f32[6]{0:T(128)} %param.17) | copy-start | bytes 76
  129.7 1.5 copy-start.1
  129.7 2.4 %copy-start.5 = (f32[2048,384]{0,1:T(8,128)S(1)}, f32[2048,384]{0,1:T(8,128)}, u32[]{:S(2)}) copy-start(f32[2048,384]{0,1:T(8,128)} %get-tuple-element.196) | copy-start | bytes 9437188
  148.1 30.7 %collective-permute-start.1 = (f32[3,384]{0,1:T(8,128)}, f32[3,384]{0,1:T(8,128)S(1)}, u32[]{:S(2)}, u32[]{:S(2)}) collective-permute-start(f32[3,384]{0,1:T(8,128)} %slice.143), channel_id=1, source_target_pairs={{4,0},{8,4},{12,8},{5,1},{9,5},{13,9},{6,2},{10,6},{14,10},{7,3},{... | collective-permute-start | bytes 13832 | tf_op jit(solution)/shard_map/ppermute | solution.py:12
  174.6 4.2 %copy-start.4 = (f32[2048,384]{0,1:T(8,128)S(1)}, f32[2048,384]{0,1:T(8,128)}, u32[]{:S(2)}) copy-start(f32[2048,384]{0,1:T(8,128)} %get-tuple-element.186) | copy-start | bytes 9437188
where the time goes:
time: 188 us; the launch traced here: 186 us
  matrix products  60.7 us (32%)
  blocking collectives  56 us (30%)
  local copies, waits for them, and re-layouts  34.3 us (18%)
  other arithmetic  27.2 us (14%)
  starting transfers between devices  6.2 us (3%)
    all_gather x1, blocking collectives, shards(): end_pieces = lax.all_gather(local_end[None], 'seq', axis=0, tiled=True)  18.7 us
    all_gather x1, blocking collectives, shards(): start_pieces = lax.all_gather(running[None], 'seq', axis=0, tiled=True)  17.3 us
    dot_general x4, matrix products, local_block(): jnp.einsum('hst,shp->thp', weights, grad_b, preferred_element_type=jnp.fl...  15.7 us
    dot_general x4, matrix products, local_block(): jnp.einsum('hts,shp->thp', weights, mixed_b, preferred_element_type=jnp.f...  15.7 us
    unnamed x46, local copies, waits for them, and re-layouts  15.7 us
    psum x1, blocking collectives, shards(): lax.psum(local_grad, 'seq') * (row_count * lax.axis_size('seq')) ** (-0.5)  10.1 us
    unnamed x1, blocking collectives  9.92 us
    dot_general x4, matrix products, local_block(): jnp.einsum('thp,tn->hpn', scaled_in, b_block, preferred_element_type=jnp....  7.97 us
  transfers between devices with their start and end apart: 2, of which 0 were waited for; matrix products, arithmetic and copies ran while one was open for 18% of the time, Pallas kernels for 0%

commit v1 on v0

--- a/solution.py
+++ b/solution.py
@@ -4,6 +4,22 @@
 from jax.sharding import PartitionSpec as P
 
 BLOCK = 512
+
+
+def threads_watch(mine, arr):
+    v_next, d_next, fresh = (jax.lax.axis_size("seq"), jax.lax.axis_index("seq"), mine.shape[0])
+    rows = [(j, (j + 1) % v_next) for j in range(v_next)]
+    grid = [(j, (j - 1) % v_next) for j in range(v_next)]
+    all_values = v_next // 2
+    before = p_next = mine
+    last = arr(mine, d_next * fresh)
+    for j0 in range(1, all_values + 1):
+        before = jax.lax.ppermute(before, axis_name="seq", perm=rows)
+        if j0 < v_next - all_values:
+            p_next = jax.lax.ppermute(p_next, perm=grid, axis_name="seq")
+            last = last + arr(p_next, (d_next + j0) % v_next * fresh)
+        last = last + arr(before, (d_next - j0) % v_next * fresh)
+    return last
 
 
 def shifted(block, axis, distance):
@@ -110,7 +126,6 @@
     prefix = jnp.cumsum(totals_all, axis=0) - totals_all
     own_prefix = lax.dynamic_slice_in_dim(prefix, position, 1, 0)[0]
     end_pieces = lax.all_gather(local_end[None], "seq", axis=0, tiled=True)
-    start_pieces = lax.all_gather(running[None], "seq", axis=0, tiled=True)
     piece_count = end_pieces.shape[0]
     sources = jnp.arange(piece_count, dtype=jnp.int32)
     from_below = (sources < position)[:, None]
@@ -122,7 +137,15 @@
         jnp.where(from_above, prefix - own_prefix[None] - device_total[None], -jnp.inf)
     )
     forward_sum = jnp.einsum("jh,jhpn->hpn", forward_weight, end_pieces, precision=highest)
-    backward_sum = jnp.einsum("jh,jhpn->hpn", backward_weight, start_pieces, precision=highest)
+    backward_sum = threads_watch(
+        running[None],
+        lambda part, offset_2: jnp.einsum(
+            "jh,jhpn->hpn",
+            lax.dynamic_slice_in_dim(backward_weight, offset_2, part.shape[0], axis=0),
+            part,
+            precision=highest,
+        ),
+    )
     before_blocks = jnp.cumsum(block_totals, axis=0) - block_totals
     after_blocks = device_total[None] - jnp.cumsum(block_totals, axis=0)
     start_states = jnp.exp(before_blocks)[:, :, None, None] * forward_sum[None] + jnp.stack(

time: 188 us -> 185 us (0.984)
  blocking collectives: 56 us -> 43.1 us
  other arithmetic: 27.2 us -> 33.2 us
  starting transfers between devices: 6.2 us -> 10.3 us
  matrix products: 60.7 us -> 58.7 us
    all_gather x1 -> x0, blocking collectives: 17.3 us -> none  [shards(): start_pieces = lax.all_gather(running[None], 'seq', axis=0, tiled=True)]
    convert_element_type x1, other arithmetic: 5.04 us -> 9.42 us  [shards(): return (layer_out, input_grad.astype(jnp.bfloat16), conv_grad)]
    ppermute x0 -> x3, starting transfers between devices: none -> 4.06 us  [the longest x1 3.21 us: threads_watch(): p_next = jax.lax.ppermute(p_next, perm=grid, axis_name='seq')]
    all_gather x1, blocking collectives: 18.7 us -> 21.1 us  [shards(): end_pieces = lax.all_gather(local_end[None], 'seq', axis=0, tiled=True)]
    psum x1, blocking collectives: 10.1 us -> 12 us  [shards(): lax.psum(local_grad, 'seq') * (row_count * lax.axis_size('seq')) ** (-0.5)]
    unnamed x46 -> x56, local copies, waits for them, and re-layouts: 15.7 us -> 15.8 us
  transfers between devices with their start and end apart: 2 -> 5, of which waited for: 0 -> 1; matrix products, arithmetic and copies ran while one was open for 18% -> 19% of each run, Pallas kernels for 0% -> 0%
where the time goes in v1:
time: 185 us; the launch traced here: 184 us
  matrix products  58.7 us (32%)
  blocking collectives  43.1 us (23%)
  local copies, waits for them, and re-layouts  35.3 us (19%)
  other arithmetic  33.2 us (18%)
  starting transfers between devices  10.3 us (6%)
    all_gather x1, blocking collectives, shards(): end_pieces = lax.all_gather(local_end[None], 'seq', axis=0, tiled=True)  21.1 us
    unnamed x56, local copies, waits for them, and re-layouts  15.8 us
    dot_general x4, matrix products, local_block(): jnp.einsum('hts,shp->thp', weights, mixed_b, preferred_element_type=jnp.f...  15.7 us
    dot_general x4, matrix products, local_block(): jnp.einsum('hst,shp->thp', weights, grad_b, preferred_element_type=jnp.fl...  15.7 us
    psum x1, blocking collectives, shards(): lax.psum(local_grad, 'seq') * (row_count * lax.axis_size('seq')) ** (-0.5)  12 us
    unnamed x1, blocking collectives  9.92 us
    convert_element_type x1, other arithmetic, shards(): return (layer_out, input_grad.astype(jnp.bfloat16), conv_grad)  9.42 us
    dot_general x4, matrix products, local_block(): jnp.einsum('thp,tn->hpn', scaled_in, b_block, preferred_element_type=jnp....  7.96 us
  transfers between devices with their start and end apart: 5, of which 1 were waited for; matrix products, arithmetic and copies ran while one was open for 19% of the time, Pallas kernels for 0%

profile of v1, /device:TPU:0, one launch (start us, length us, event | category | flops | bytes accessed | tf_op | source)
XLA Modules:
  0.0 183.8 jit_solution(16388418348041469794)
XLA Ops:
  2.2 4.9 %collective-permute-start = (bf16[3,384]{0,1:T(8,128)(2,1)}, bf16[3,384]{0,1:T(8,128)(2,1)S(1)}, u32[]{:S(2)}, u32[]{:S(2)}) collective-permute-start(bf16[3,384]{0,1:T(8,128)(2,1)} %copy.102), channel_id=1, source_target_pairs={{0,4},{4,8},{8,12},{1,5},{5,9},{9,13},{2,6},{6,10},{10,14},{3,7},{... | collective-permute-start | bytes 6920 | tf_op jit(solution)/shard_map/ppermute | solution.py:28
  9.5 7.2 %reduce-window.6 = f32[6,4,4,128]{3,2,1,0:T(4,128)S(1)} reduce-window(f32[6,4,4,128]{3,2,1,0:T(4,128)S(1)} %reshape.149, f32[]{:T(128)} %constant.72.clone.1), window={size=1x1x1x128 pad=0_0x0_0x0_0x127_0}, to_apply=%region_0.1 | reduce-window | flops 1560576 | bytes 98308 | tf_op jit(solution)/shard_map/reduce-window
  19.5 1.2 dynamic-slice
  21.7 9.9 %all-reduce = f32[24]{0:T(128)S(1)} all-reduce(f32[24]{0:T(128)S(1)} %dynamic-update-slice), channel_id=2, replica_groups=mesh['groups'=2,'seq'=4,'head'=2,'sub'=2] {'seq'}, use_global_device_ids=true, to_apply=%add | all-reduce | flops 24 | bytes 192
  33.6 1.7 copy.103
  35.4 1.6 copy.108
  37.0 2.9 %reshape.152 = bf16[4,512,6,64]{1,0,3,2:T(4,128)(2,1)S(1)} reshape(bf16[2048,384]{0,1:T(8,128)(2,1)} %copy.108) | data formatting | bytes 3145728 | tf_op jit(solution)/shard_map/reshape | solution.py:67
  39.9 1.7 copy.112
  43.5 4.2 %multiply_convert_fusion.13 = (bf16[2048,384]{0,1:T(8,128)(2,1)}, f32[2048,384]{0,1:T(8,128)}) fusion(bf16[2048,384]{0,1:T(8,128)(2,1)S(1)} %copy.103, f32[384]{0:T(512)S(1)} %get-tuple-element.162, bf16[3,384]{0,1:T(8,128)(2,1)S(1)} %collective-permute-done, f32[384]{0:T(512)S(1)} %get-tuple-element.163, f32[384]{0:T(512)S(1)} %get-tuple-element.161, ...), kind=kLoop, calls=%fused_computation.84 | loop fusion | flops 19660800 | bytes 6299904 | tf_op jit(solution)/shard_map/convert_element_type | solution.py:56
  47.7 2.9 %reshape.146 = bf16[4,512,6,64]{1,0,3,2:T(4,128)(2,1)S(1)} reshape(bf16[2048,384]{0,1:T(8,128)(2,1)} %get-tuple-element.195) | data formatting | bytes 3145728 | tf_op jit(solution)/shard_map/reshape | solution.py:66
  50.6 1.7 copy.105
  52.3 55.5 %while.17 = (s32[]{:T(128)}, f32[4,512,6,64]{1,3,2,0:T(8,128)}, f32[4,512,6,64]{1,3,2,0:T(8,128)}, f32[4,6,64,128]{3,2,1,0:T(8,128)}, f32[4,6,64,128]{3,2,1,0:T(...) while((s32[]{:T(128)}, f32[4,512,6,64]{1,3,2,0:T(8,128)}, ...), condition=%wide.region_3.4_spmd.clone, body=%wide.region_2.3_spmd.clone.sunk | while | flops 587601920 | bytes 8370377 | solution.py:98
  52.4 1.3 fusion.111
  53.7 3.9 %fusion.112 = f32[4,512,6,64]{1,3,2,0:T(8,128)} fusion(f32[4,512,6,64]{1,3,2,0:T(8,128)} %get-tuple-element.313, s32[]{:T(128)S(6)} %copy.162, f32[6,512]{1,0:T(8,128)S(1)} %bitcast.199, f32[6,512]{1,0:T(8,128)S(1)} %bitcast.201, f32[512,512]{1,0:T(8,128)S(1)} %fusion.111, pred[512,512]{1,0:T(8,128)(4,1)S(1)} %iota_compare_fusion.4, ...), kind=kOutput, calls=%fused_computation.5.clone.1 | convolution fusion | flops 209190912 | bytes 2540544 | tf_op jit(solution)/shard_map/while/body/eval_jaxpr/hts,shp->thp/dot_general | solution.py:78
  57.6 3.9 %fusion.113 = f32[4,512,6,64]{1,3,2,0:T(8,128)} fusion(f32[4,512,6,64]{1,3,2,0:T(8,128)} %get-tuple-element.314, s32[]{:T(128)S(6)} %copy.162, f32[6,512]{1,0:T(8,128)S(1)} %bitcast.200, f32[6,512]{1,0:T(8,128)S(1)} %bitcast.202, f32[512,512]{1,0:T(8,128)S(1)} %fusion.111, pred[512,512]{1,0:T(8,128)(4,1)S(1)} %iota_compare_fusion.4, ...), kind=kOutput, calls=%fused_computation.7.clone.1 | convolution fusion | flops 209190912 | bytes 2540544 | tf_op jit(solution)/shard_map/while/body/eval_jaxpr/hst,shp->thp/dot_general | solution.py:81
  62.1 2.0 %fusion.114 = f32[4,6,64,128]{3,2,1,0:T(8,128)} fusion(f32[4,6,64,128]{3,2,1,0:T(8,128)} %get-tuple-element.315, s32[]{:T(128)S(6)} %copy.162, f32[512,6]{0,1:T(8,128)S(1)} %copy.151, bf16[4,512,6,64]{1,3,2,0:T(8,128)(2,1)} %get-tuple-element.329, bf16[4,512,128]{2,1,0:T(8,128)(2,1)} %get-tuple-element.331), kind=kOutput, calls=%fused_computation.11.clone.1 | convolution fusion | flops 50921472 | bytes 734720 | tf_op jit(solution)/shard_map/while/body/eval_jaxpr/thp,tn->hpn/dot_general | solution.py:87
  64.2 2.0 %fusion.115 = f32[4,6,64,128]{3,2,1,0:T(8,128)} fusion(f32[4,6,64,128]{3,2,1,0:T(8,128)} %get-tuple-element.316, s32[]{:T(128)S(6)} %copy.162, f32[512,6]{0,1:T(8,128)S(1)} %copy.152, bf16[4,512,6,64]{1,3,2,0:T(8,128)(2,1)} %get-tuple-element.334, bf16[4,512,128]{2,1,0:T(8,128)(2,1)} %get-tuple-element.330), kind=kOutput, calls=%fused_computation.9.clone.1 | convolution fusion | flops 50921472 | bytes 734720 | tf_op jit(solution)/shard_map/while/body/eval_jaxpr/thp,tn->hpn/dot_general | solution.py:93
  66.2 1.3 fusion.111
  67.6 3.9 %fusion.112 = f32[4,512,6,64]{1,3,2,0:T(8,128)} fusion(f32[4,512,6,64]{1,3,2,0:T(8,128)} %get-tuple-element.313, s32[]{:T(128)S(6)} %copy.162, f32[6,512]{1,0:T(8,128)S(1)} %bitcast.199, f32[6,512]{1,0:T(8,128)S(1)} %bitcast.201, f32[512,512]{1,0:T(8,128)S(1)} %fusion.111, pred[512,512]{1,0:T(8,128)(4,1)S(1)} %iota_compare_fusion.4, ...), kind=kOutput, calls=%fused_computation.5.clone.1 | convolution fusion | flops 209190912 | bytes 2540544 | tf_op jit(solution)/shard_map/while/body/eval_jaxpr/hts,shp->thp/dot_general | solution.py:78
  71.5 3.9 %fusion.113 = f32[4,512,6,64]{1,3,2,0:T(8,128)} fusion(f32[4,512,6,64]{1,3,2,0:T(8,128)} %get-tuple-element.314, s32[]{:T(128)S(6)} %copy.162, f32[6,512]{1,0:T(8,128)S(1)} %bitcast.200, f32[6,512]{1,0:T(8,128)S(1)} %bitcast.202, f32[512,512]{1,0:T(8,128)S(1)} %fusion.111, pred[512,512]{1,0:T(8,128)(4,1)S(1)} %iota_compare_fusion.4, ...), kind=kOutput, calls=%fused_computation.7.clone.1 | convolution fusion | flops 209190912 | bytes 2540544 | tf_op jit(solution)/shard_map/while/body/eval_jaxpr/hst,shp->thp/dot_general | solution.py:81
  75.9 2.0 %fusion.114 = f32[4,6,64,128]{3,2,1,0:T(8,128)} fusion(f32[4,6,64,128]{3,2,1,0:T(8,128)} %get-tuple-element.315, s32[]{:T(128)S(6)} %copy.162, f32[512,6]{0,1:T(8,128)S(1)} %copy.151, bf16[4,512,6,64]{1,3,2,0:T(8,128)(2,1)} %get-tuple-element.329, bf16[4,512,128]{2,1,0:T(8,128)(2,1)} %get-tuple-element.331), kind=kOutput, calls=%fused_computation.11.clone.1 | convolution fusion | flops 50921472 | bytes 734720 | tf_op jit(solution)/shard_map/while/body/eval_jaxpr/thp,tn->hpn/dot_general | solution.py:87
  78.0 2.0 %fusion.115 = f32[4,6,64,128]{3,2,1,0:T(8,128)} fusion(f32[4,6,64,128]{3,2,1,0:T(8,128)} %get-tuple-element.316, s32[]{:T(128)S(6)} %copy.162, f32[512,6]{0,1:T(8,128)S(1)} %copy.152, bf16[4,512,6,64]{1,3,2,0:T(8,128)(2,1)} %get-tuple-element.334, bf16[4,512,128]{2,1,0:T(8,128)(2,1)} %get-tuple-element.330), kind=kOutput, calls=%fused_computation.9.clone.1 | convolution fusion | flops 50921472 | bytes 734720 | tf_op jit(solution)/shard_map/while/body/eval_jaxpr/thp,tn->hpn/dot_general | solution.py:93
  80.0 1.3 fusion.111
  81.4 4.0 %fusion.112 = f32[4,512,6,64]{1,3,2,0:T(8,128)} fusion(f32[4,512,6,64]{1,3,2,0:T(8,128)} %get-tuple-element.313, s32[]{:T(128)S(6)} %copy.162, f32[6,512]{1,0:T(8,128)S(1)} %bitcast.199, f32[6,512]{1,0:T(8,128)S(1)} %bitcast.201, f32[512,512]{1,0:T(8,128)S(1)} %fusion.111, pred[512,512]{1,0:T(8,128)(4,1)S(1)} %iota_compare_fusion.4, ...), kind=kOutput, calls=%fused_computation.5.clone.1 | convolution fusion | flops 209190912 | bytes 2540544 | tf_op jit(solution)/shard_map/while/body/eval_jaxpr/hts,shp->thp/dot_general | solution.py:78
  85.3 3.9 %fusion.113 = f32[4,512,6,64]{1,3,2,0:T(8,128)} fusion(f32[4,512,6,64]{1,3,2,0:T(8,128)} %get-tuple-element.314, s32[]{:T(128)S(6)} %copy.162, f32[6,512]{1,0:T(8,128)S(1)} %bitcast.200, f32[6,512]{1,0:T(8,128)S(1)} %bitcast.202, f32[512,512]{1,0:T(8,128)S(1)} %fusion.111, pred[512,512]{1,0:T(8,128)(4,1)S(1)} %iota_compare_fusion.4, ...), kind=kOutput, calls=%fused_computation.7.clone.1 | convolution fusion | flops 209190912 | bytes 2540544 | tf_op jit(solution)/shard_map/while/body/eval_jaxpr/hst,shp->thp/dot_general | solution.py:81
  89.8 2.0 %fusion.114 = f32[4,6,64,128]{3,2,1,0:T(8,128)} fusion(f32[4,6,64,128]{3,2,1,0:T(8,128)} %get-tuple-element.315, s32[]{:T(128)S(6)} %copy.162, f32[512,6]{0,1:T(8,128)S(1)} %copy.151, bf16[4,512,6,64]{1,3,2,0:T(8,128)(2,1)} %get-tuple-element.329, bf16[4,512,128]{2,1,0:T(8,128)(2,1)} %get-tuple-element.331), kind=kOutput, calls=%fused_computation.11.clone.1 | convolution fusion | flops 50921472 | bytes 734720 | tf_op jit(solution)/shard_map/while/body/eval_jaxpr/thp,tn->hpn/dot_general | solution.py:87
  91.9 2.0 %fusion.115 = f32[4,6,64,128]{3,2,1,0:T(8,128)} fusion(f32[4,6,64,128]{3,2,1,0:T(8,128)} %get-tuple-element.316, s32[]{:T(128)S(6)} %copy.162, f32[512,6]{0,1:T(8,128)S(1)} %copy.152, bf16[4,512,6,64]{1,3,2,0:T(8,128)(2,1)} %get-tuple-element.334, bf16[4,512,128]{2,1,0:T(8,128)(2,1)} %get-tuple-element.330), kind=kOutput, calls=%fused_computation.9.clone.1 | convolution fusion | flops 50921472 | bytes 734720 | tf_op jit(solution)/shard_map/while/body/eval_jaxpr/thp,tn->hpn/dot_general | solution.py:93
  93.9 1.3 fusion.111
  95.3 3.9 %fusion.112 = f32[4,512,6,64]{1,3,2,0:T(8,128)} fusion(f32[4,512,6,64]{1,3,2,0:T(8,128)} %get-tuple-element.313, s32[]{:T(128)S(6)} %copy.162, f32[6,512]{1,0:T(8,128)S(1)} %bitcast.199, f32[6,512]{1,0:T(8,128)S(1)} %bitcast.201, f32[512,512]{1,0:T(8,128)S(1)} %fusion.111, pred[512,512]{1,0:T(8,128)(4,1)S(1)} %iota_compare_fusion.4, ...), kind=kOutput, calls=%fused_computation.5.clone.1 | convolution fusion | flops 209190912 | bytes 2540544 | tf_op jit(solution)/shard_map/while/body/eval_jaxpr/hts,shp->thp/dot_general | solution.py:78
  99.2 4.0 %fusion.113 = f32[4,512,6,64]{1,3,2,0:T(8,128)} fusion(f32[4,512,6,64]{1,3,2,0:T(8,128)} %get-tuple-element.314, s32[]{:T(128)S(6)} %copy.162, f32[6,512]{1,0:T(8,128)S(1)} %bitcast.200, f32[6,512]{1,0:T(8,128)S(1)} %bitcast.202, f32[512,512]{1,0:T(8,128)S(1)} %fusion.111, pred[512,512]{1,0:T(8,128)(4,1)S(1)} %iota_compare_fusion.4, ...), kind=kOutput, calls=%fused_computation.7.clone.1 | convolution fusion | flops 209190912 | bytes 2540544 | tf_op jit(solution)/shard_map/while/body/eval_jaxpr/hst,shp->thp/dot_general | solution.py:81
  103.7 2.0 %fusion.114 = f32[4,6,64,128]{3,2,1,0:T(8,128)} fusion(f32[4,6,64,128]{3,2,1,0:T(8,128)} %get-tuple-element.315, s32[]{:T(128)S(6)} %copy.162, f32[512,6]{0,1:T(8,128)S(1)} %copy.151, bf16[4,512,6,64]{1,3,2,0:T(8,128)(2,1)} %get-tuple-element.329, bf16[4,512,128]{2,1,0:T(8,128)(2,1)} %get-tuple-element.331), kind=kOutput, calls=%fused_computation.11.clone.1 | convolution fusion | flops 50921472 | bytes 734720 | tf_op jit(solution)/shard_map/while/body/eval_jaxpr/thp,tn->hpn/dot_general | solution.py:87
  105.8 2.0 %fusion.115 = f32[4,6,64,128]{3,2,1,0:T(8,128)} fusion(f32[4,6,64,128]{3,2,1,0:T(8,128)} %get-tuple-element.316, s32[]{:T(128)S(6)} %copy.162, f32[512,6]{0,1:T(8,128)S(1)} %copy.152, bf16[4,512,6,64]{1,3,2,0:T(8,128)(2,1)} %get-tuple-element.334, bf16[4,512,128]{2,1,0:T(8,128)(2,1)} %get-tuple-element.330), kind=kOutput, calls=%fused_computation.9.clone.1 | convolution fusion | flops 50921472 | bytes 734720 | tf_op jit(solution)/shard_map/while/body/eval_jaxpr/thp,tn->hpn/dot_general | solution.py:93
  107.9 2.6 %slice_add_fusion = (f32[1,6,64,128]{3,2,1,0:T(8,128)S(1)}, f32[1,6,64,128]{3,2,1,0:T(8,128)}, f32[1,6,64,128]{3,2,1,0:T(8,128)}, f32[1,6,64,128]{3,2,1,0:T(8,12...) fusion(f32[4,6,64,128]{3,2,1,0:T(8,128)} %get-tuple-element.71,, ...), kind=kLoop, calls=%fused_computation.108 | loop fusion | flops 688128 | bytes 3145872 | tf_op jit(solution)/shard_map/add | solution.py:119
  111.0 3.2 %collective-permute-start.1 = (f32[1,6,64,128]{3,2,1,0:T(8,128)S(1)}, f32[1,6,64,128]{3,2,1,0:T(8,128)}, u32[]{:S(2)}, u32[]{:S(2)}) collective-permute-start(f32[1,6,64,128]{3,2,1,0:T(8,128)S(1)} %get-tuple-element.187), channel_id=1, source_target_pairs={{0,12},{4,0},{8,4},{12,8},{1,13},{5,1},{9,5},{13,9},{2,14},{6,2},{... | collective-permute-start | bytes 589832 | tf_op jit(solution)/shard_map/ppermute | solution.py:19
  114.2 21.1 %all_gather.7 = f32[4,6,64,128]{3,2,1,0:T(8,128)S(1)} all-gather(f32[1,6,64,128]{3,2,1,0:T(8,128)S(1)} %get-tuple-element.215), channel_id=1, replica_groups=mesh['groups'=2,'seq'=4,'head'=2,'sub'=2] {'seq'}, dimensions={0}, use_global_device_ids=true | all-gather | bytes 983040 | tf_op jit(solution)/shard_map/all_gather | solution.py:128
  135.4 1.8 fusion.62
  140.0 1.6 copy.131
  141.5 2.6 %copy.120 = bf16[2048,384]{1,0:T(8,128)(2,1)} copy(bf16[2048,384]{0,1:T(8,128)(2,1)} %bitcast.193) | data formatting | bytes 3145728
  145.2 1.2 fusion.70
  146.5 3.3 %fusion.55 = f32[4,512,6,64]{1,3,2,0:T(8,128)S(1)} fusion(f32[4,512,6,64]{1,3,2,0:T(8,128)} %get-tuple-element.70, bf16[4,512,128,1]{2,1,3,0:T(8,128)(2,1)} %bitcast.191, f32[4,512,6]{1,2,0:T(8,128)} %copy.118, f32[6]{0:T(128)} %param.17, f32[1,6,64,128]{3,2,1,0:T(8,128)S(1)} %broadcast.80, f32[1,6,64,128]{3,2,1,0:T(8,128)} %get-tuple-element.190, ...), kind=kOutput, calls=%fused_computation.79 | convolution fusion | flops 206438400 | bytes 9420920 | tf_op jit(solution)/shard_map/btn,bhpn->bthp/dot_general | solution.py:170
  149.8 2.0 %copy.119 = f32[4,512,6,64]{1,0,3,2:T(4,128)S(1)} copy(f32[4,512,6,64]{1,3,2,0:T(8,128)S(1)} %fusion.55) | data formatting | bytes 6291456 | tf_op jit(solution)/shard_map/add | solution.py:177
  151.9 1.5 copy.132
  153.8 3.3 %fusion.50 = (f32[384]{0:T(512)S(1)}, f32[384]{0:T(512)S(1)}, f32[384]{0:T(512)S(1)}, f32[384]{0:T(512)S(1)}, f32[2048,384]{0,1:T(8,128)S(1)}) fusion(bf16[2048,384]{0,1:T(8,128)(2,1)S(1)} %copy.103, bf16[3,384]{0,1:T(8,128)(2,1)S(1)} %copy-done.10, f32[2048,384]{0,1:T(8,128)S(1)} %copy-done.5, f32[2048,384]{0,1:T(8,128)S(1)} %bitcast.187), kind=kLoop, calls=%fused_computation.72 | loop fusion | flops 22804992 | bytes 11018496 | tf_op jit(solution)/shard_map/reduce_sum | solution.py:191
  157.1 1.7 copy-done.4
  158.8 1.3 collective-permute-start.4
  160.1 12.0 %psum.7 = f32[4,384]{1,0:T(4,128)S(1)} all-reduce(f32[4,384]{1,0:T(4,128)S(1)} %pad_maximum_fusion.2), channel_id=1, replica_groups=mesh['groups'=2,'seq'=4,'head'=2,'sub'=2] {'seq'}, use_global_device_ids=true, to_apply=%region_11.12 | all-reduce | flops 1536 | bytes 12288 | tf_op jit(solution)/shard_map/psum | solution.py:195
  172.8 9.4 %fusion.44 = bf16[2048,384]{0,1:T(8,128)(2,1)S(1)} fusion(f32[2048,384]{0,1:T(8,128)} %copy-done.4, f32[3,384]{0,1:T(8,128)S(1)} %collective-permute-done.4, f32[384]{0:T(512)S(1)} %get-tuple-element.162, f32[384]{0:T(512)S(1)} %get-tuple-element.163, f32[384]{0:T(512)S(1)} %get-tuple-element.161, f32[384]{0:T(512)S(1)} %get-tuple-element.160), kind=kLoop, calls=%fused_computation.66 | loop fusion | flops 8650752 | bytes 4729344 | tf_op jit(solution)/shard_map/convert_element_type | solution.py:196
  182.2 1.6 copy.121
  (140 shorter events, 19.1 us)
Async XLA Ops:
  0.6 34.7 %copy-start.8 = (bf16[2048,384]{1,0:T(8,128)(2,1)S(1)}, bf16[2048,384]{1,0:T(8,128)(2,1)}, u32[]{:S(2)}) copy-start(bf16[2048,384]{1,0:T(8,128)(2,1)} %param.19) | copy-start | bytes 4718596
  2.2 41.2 %collective-permute-start = (bf16[3,384]{0,1:T(8,128)(2,1)}, bf16[3,384]{0,1:T(8,128)(2,1)S(1)}, u32[]{:S(2)}, u32[]{:S(2)}) collective-permute-start(bf16[3,384]{0,1:T(8,128)(2,1)} %copy.102), channel_id=1, source_target_pairs={{0,4},{4,8},{8,12},{1,5},{5,9},{9,13},{2,6},{6,10},{10,14},{3,7},{... | collective-permute-start | bytes 6920 | tf_op jit(solution)/shard_map/ppermute | solution.py:28
  18.3 15.3 %copy-start.14 = (f32[6]{0:T(128)}, f32[6]{0:T(128)S(1)}, u32[]{:S(2)}) copy-start(f32[6]{0:T(128)S(1)} %get-tuple-element.156) | copy-start | bytes 76
  18.3 15.3 %copy-start.16 = (f32[6]{0:T(128)}, f32[6]{0:T(128)S(1)}, u32[]{:S(2)}) copy-start(f32[6]{0:T(128)S(1)} %get-tuple-element.157) | copy-start | bytes 76
  39.9 7.8 %copy-start.2 = (bf16[4,512,6,64]{1,0,3,2:T(4,128)(2,1)}, bf16[4,512,6,64]{1,0,3,2:T(4,128)(2,1)S(1)}, u32[]{:S(2)}) copy-start(bf16[4,512,6,64]{1,0,3,2:T(4,128)(2,1)S(1)} %reshape.152) | copy-start | bytes 4718596
  43.5 4.2 %copy-start.9 = (bf16[3,384]{0,1:T(8,128)(2,1)}, bf16[3,384]{0,1:T(8,128)(2,1)S(1)}, u32[]{:S(2)}) copy-start(bf16[3,384]{0,1:T(8,128)(2,1)S(1)} %collective-permute-done) | copy-start | bytes 6916
  50.6 1.7 copy-start
  52.2 55.6 %copy-start.15 = (f32[6]{0:T(128)S(1)}, f32[6]{0:T(128)}, u32[]{:S(2)}) copy-start(f32[6]{0:T(128)} %copy-done.14) | copy-start | bytes 76
  52.2 55.6 %copy-start.17 = (f32[6]{0:T(128)S(1)}, f32[6]{0:T(128)}, u32[]{:S(2)}) copy-start(f32[6]{0:T(128)} %copy-done.16) | copy-start | bytes 76
  52.2 55.6 %copy-start.18 = (f32[6]{0:T(128)S(1)}, f32[6]{0:T(128)}, u32[]{:S(2)}) copy-start(f32[6]{0:T(128)} %get-tuple-element.158) | copy-start | bytes 76
  52.2 55.6 %copy-start.19 = (f32[6]{0:T(128)S(1)}, f32[6]{0:T(128)}, u32[]{:S(2)}) copy-start(f32[6]{0:T(128)} %get-tuple-element.159) | copy-start | bytes 76
  52.2 55.6 %copy-start.20 = (f32[6]{0:T(128)S(1)}, f32[6]{0:T(128)}, u32[]{:S(2)}) copy-start(f32[6]{0:T(128)} %get-tuple-element.221) | copy-start | bytes 76
  52.3 55.6 %copy-start.21 = (f32[6]{0:T(128)S(1)}, f32[6]{0:T(128)}, u32[]{:S(2)}) copy-start(f32[6]{0:T(128)} %get-tuple-element.222) | copy-start | bytes 76
  52.3 83.1 %copy-start.12 = (f32[4,6,1,1]{0,2,3,1:T(1,128)S(1)}, f32[4,6,1,1]{0,2,3,1:T(1,128)}, u32[]{:S(2)}) copy-start(f32[4,6,1,1]{0,2,3,1:T(1,128)} %copy.122) | copy-start | bytes 292
  107.8 29.7 %copy-start.1 = (bf16[4,512,6,64]{1,0,3,2:T(4,128)(2,1)S(1)}, bf16[4,512,6,64]{1,0,3,2:T(4,128)(2,1)}, u32[]{:S(2)}) copy-start(bf16[4,512,6,64]{1,0,3,2:T(4,128)(2,1)} %copy-done) | copy-start | bytes 4718596
  107.8 29.7 %copy-start.6 = (bf16[4,512,128]{2,1,0:T(8,128)(2,1)S(1)}, bf16[4,512,128]{2,1,0:T(8,128)(2,1)}, u32[]{:S(2)}) copy-start(bf16[4,512,128]{2,1,0:T(8,128)(2,1)} %get-tuple-element.336) | copy-start | bytes 1572868
  107.8 29.7 %copy-start.7 = (f32[4,512,6,64]{1,3,2,0:T(8,128)S(1)}, f32[4,512,6,64]{1,3,2,0:T(8,128)}, u32[]{:S(2)}) copy-start(f32[4,512,6,64]{1,3,2,0:T(8,128)} %get-tuple-element.68) | copy-start | bytes 9437188
  107.8 29.7 %copy-start.11 = (f32[4,512,6]{1,2,0:T(8,128)S(1)}, f32[4,512,6]{1,2,0:T(8,128)}, u32[]{:S(2)}) copy-start(f32[4,512,6]{1,2,0:T(8,128)} %copy.114) | copy-start | bytes 147460
  107.8 29.7 %copy-start.13 = (f32[4,6]{1,0:T(4,128)S(1)}, f32[4,6]{1,0:T(4,128)}, u32[]{:S(2)}) copy-start(f32[4,6]{1,0:T(4,128)} %get-tuple-element.210) | copy-start | bytes 292
  107.8 29.7 %copy-start.22 = (f32[6]{0:T(128)S(1)}, f32[6]{0:T(128)}, u32[]{:S(2)}) copy-start(f32[6]{0:T(128)} %param.17) | copy-start | bytes 76
  110.4 26.8 %collective-permute-start.2 = (f32[1,6,64,128]{3,2,1,0:T(8,128)S(1)}, f32[1,6,64,128]{3,2,1,0:T(8,128)}, u32[]{:S(2)}, u32[]{:S(2)}) collective-permute-start(f32[1,6,64,128]{3,2,1,0:T(8,128)S(1)} %get-tuple-element.187), channel_id=1, source_target_pairs={{0,4},{4,8},{8,12},{12,0},{1,5},{5,9},{9,13},{13,1},{2,6},{6,10},{... | collective-permute-start | bytes 589832 | tf_op jit(solution)/shard_map/ppermute | solution.py:17
  111.0 33.1 %collective-permute-start.1 = (f32[1,6,64,128]{3,2,1,0:T(8,128)S(1)}, f32[1,6,64,128]{3,2,1,0:T(8,128)}, u32[]{:S(2)}, u32[]{:S(2)}) collective-permute-start(f32[1,6,64,128]{3,2,1,0:T(8,128)S(1)} %get-tuple-element.187), channel_id=1, source_target_pairs={{0,12},{4,0},{8,4},{12,8},{1,13},{5,1},{9,5},{13,9},{2,14},{6,2},{... | collective-permute-start | bytes 589832 | tf_op jit(solution)/shard_map/ppermute | solution.py:19
  137.2 8.0 %collective-permute-start.3 = (f32[1,6,64,128]{3,2,1,0:T(8,128)}, f32[1,6,64,128]{3,2,1,0:T(8,128)}, u32[]{:S(2)}, u32[]{:S(2)}) collective-permute-start(f32[1,6,64,128]{3,2,1,0:T(8,128)} %collective-permute-done.2), channel_id=1, source_target_pairs={{0,4},{4,8},{8,12},{12,0},{1,5},{5,9},{9,13},{13,1},{2,6},{6,10},{... | collective-permute-start | bytes 589832 | tf_op jit(solution)/shard_map/ppermute | solution.py:17
  139.9 6.6 %copy-start.3 = (bf16[4,512,6,64]{1,0,3,2:T(4,128)(2,1)S(1)}, bf16[4,512,6,64]{1,0,3,2:T(4,128)(2,1)}, u32[]{:S(2)}) copy-start(bf16[4,512,6,64]{1,0,3,2:T(4,128)(2,1)} %copy-done.2) | copy-start | bytes 4718596
  151.9 1.9 %copy-start.5 = (f32[2048,384]{0,1:T(8,128)S(1)}, f32[2048,384]{0,1:T(8,128)}, u32[]{:S(2)}) copy-start(f32[2048,384]{0,1:T(8,128)} %get-tuple-element.196) | copy-start | bytes 9437188
  151.9 1.9 %copy-start.10 = (bf16[3,384]{0,1:T(8,128)(2,1)S(1)}, bf16[3,384]{0,1:T(8,128)(2,1)}, u32[]{:S(2)}) copy-start(bf16[3,384]{0,1:T(8,128)(2,1)} %copy-done.9) | copy-start | bytes 6916
  157.1 1.7 copy-start.4
  158.8 14.0 %collective-permute-start.4 = (f32[3,384]{0,1:T(8,128)S(1)}, f32[3,384]{0,1:T(8,128)S(1)}, u32[]{:S(2)}, u32[]{:S(2)}) collective-permute-start(f32[3,384]{0,1:T(8,128)S(1)} %slice.143), channel_id=1, source_target_pairs={{4,0},{8,4},{12,8},{5,1},{9,5},{13,9},{6,2},{10,6},{14,10},{7,3},{... | collective-permute-start | bytes 13832 | tf_op jit(solution)/shard_map/ppermute | solution.py:28
